TPU v7x, 128 devices: a whole 4x4x4 slice. The times are simulated.
128 devices in a mesh: dp: 2 (over core), tensor: 64 (over x, z, y).
Axes of the slice: x: 4, y: 4, z: 4, core: 2. Of those that a mesh axis runs over, the one named last changes fastest.
Arguments:
- hidden: bfloat16 [2048, 4096], P(('dp', 'tensor')), parts along dimension 0
- norm_gain: float32 [4096], replicated, may hold values from 0.3 to 3
- head_weight: bfloat16 [256512, 4096], P(('dp', 'tensor')), parts along dimension 0
- targets: int32 [2048], P(('dp', 'tensor')), parts along dimension 0, may hold values from 0 to 128255
- lengths: int32 [24], P('dp'), parts along dimension 0, may hold values from 1 to 256, as said below
- offsets: int32 [24], P('dp'), parts along dimension 0, may hold values from 0 to 1023, as said below
- loss_mask: int32 [2048], P(('dp', 'tensor')), parts along dimension 0, may hold values from 0 to 1, as said below
Outputs:
- token_logprob: float32 [2048], P(('dp', 'tensor')), parts along dimension 0
- token_entropy: float32 [2048], P(('dp', 'tensor')), parts along dimension 0
- sequence_score: float32 [24], P('dp'), parts along dimension 0
There are 2 independent parts, one for each index of `dp`. A program takes and returns all parts, laid end to end along the dimension named above; an argument that names none is the same for every part. Nothing has to cross between parts.
Inputs may be any that keep to these rules, and one draw needn't show every extreme that they name: `lengths`: responses lie in order and do not intersection within the 1024 rows; one has length exactly 256. offsets[k] + lengths[k] <= offsets[k+1], and the last response ends within the pack. `loss_mask`: ones only inside responses; the 16 rows of one index of tensor hold at most 10 ones, exactly 10 on some index.
All inputs are finite; a program needn't handle non-finite values.
Results may differ from a plain program's by a relative error of at most 0.0065.
The roundings to bfloat16 on the way count: a program that leaves them out, or rounds other values in their place, can miss the bound.
Values may be sent and summed in bfloat16 or wider, within the bound.
No kernel may reach another device: no remote copies, remote signals or barrier semaphores. Data moves between devices by JAX's collectives and lax.ppermute only.
A program may use at most 128 MiB of HBM per device.

v0:
```python
import jax
import jax.numpy as jnp
from jax import lax
from jax.sharding import PartitionSpec as P

epsilon = 1e-05


def row_stats(gathered, gathered_ids, head_weight, vocab_start):
    peaks, sums, spreads, pickeds = ([], [], [], [])
    for row_begin in range(0, gathered.shape[0], 512):
        row_block = gathered[row_begin : row_begin + 512]
        block_ids = gathered_ids[row_begin : row_begin + 512]
        scores = lax.dot_general(
            head_weight, row_block, (((1,), (1,)), ((), ())), preferred_element_type=jnp.float32
        )
        row_peak = jnp.max(scores, axis=0)
        centred = scores - row_peak[None, :]
        expo = jnp.exp(centred)
        sums.append(jnp.sum(expo, axis=0))
        spreads.append(jnp.sum(expo * centred, axis=0))
        column = vocab_start + lax.broadcasted_iota(jnp.int32, scores.shape, 0)
        pickeds.append(jnp.sum(jnp.where(column == block_ids[None, :], scores, 0.0), axis=0))
        peaks.append(row_peak)
    return (
        jnp.concatenate(peaks),
        jnp.concatenate(sums),
        jnp.concatenate(spreads),
        jnp.concatenate(pickeds),
    )


def rescaled(row_peak, row_sum, row_spread, global_peak):
    shift_by = row_peak - global_peak
    factor = jnp.exp(shift_by)
    return (factor * row_sum, factor * (row_spread + shift_by * row_sum))


def local(hidden, norm_gain, head_weight, targets, lengths, offsets, loss_mask):
    own_rows = hidden.shape[0]
    values = hidden.astype(jnp.float32)
    meansq = jnp.mean(values * values, axis=1, keepdims=True)
    normed = (values * lax.rsqrt(meansq + epsilon) * norm_gain[None, :]).astype(jnp.bfloat16)
    width = normed.shape[0]
    gathered, gathered_ids = (
        lax.all_gather(normed, "tensor", axis=0, tiled=True),
        lax.all_gather(targets, "tensor", axis=0, tiled=True),
    )
    shard_index = lax.axis_index("tensor")
    vocab_start = shard_index * head_weight.shape[0]
    row_peak, row_sum, row_spread, picked = row_stats(
        gathered, gathered_ids, head_weight, vocab_start
    )
    own_start = shard_index * width
    global_peak = lax.pmax(row_peak, "tensor")
    scaled_sum, scaled_spread = rescaled(row_peak, row_sum, row_spread, global_peak)
    summed = lax.psum((scaled_sum, scaled_spread, picked), "tensor")
    sum_exp, spread, target_logit = [
        lax.dynamic_slice_in_dim(item, own_start, width) for item in summed
    ]
    final_peak = lax.dynamic_slice_in_dim(global_peak, own_start, width)
    log_total = jnp.log(sum_exp)
    logprob_rows = target_logit - final_peak - log_total
    entropy_rows = log_total - spread / sum_exp
    mask_float = loss_mask.astype(jnp.float32)
    token_logprob = logprob_rows * mask_float
    token_entropy = entropy_rows * mask_float
    positions = shard_index * own_rows + lax.broadcasted_iota(jnp.int32, (own_rows,), 0)
    inside = (positions[None, :] >= offsets[:, None]) & (
        positions[None, :] < (offsets + lengths)[:, None]
    )
    partial_sums = jnp.sum(jnp.where(inside, token_logprob[None, :], 0.0), axis=1)
    seq_totals = lax.psum(partial_sums, "tensor")
    sequence_score = seq_totals / lengths.astype(jnp.float32)
    return (token_logprob, token_entropy, sequence_score)


def solution(mesh):
    return jax.shard_map(
        local,
        mesh=mesh,
        in_specs=(
            P(("dp", "tensor"), None),
            P(),
            P(("dp", "tensor"), None),
            P(("dp", "tensor")),
            P("dp"),
            P("dp"),
            P(("dp", "tensor")),
        ),
        out_specs=(P(("dp", "tensor")), P(("dp", "tensor")), P("dp")),
        check_vma=False,
    )
```

profile of v0, /device:TPU:0, one launch (start us, length us, event | category | flops | bytes accessed | tf_op | source)
XLA Modules:
  0.0 659.3 jit_solution(6251111973607725108)
XLA Ops:
  7.2 0.0 all-gather.2.cloned.1.call-start
  7.2 1.1 fusion.8
  8.3 1.7 fusion.10
  9.9 0.0 all-gather.2.cloned.1.call-update
  10.0 1.2 dynamic-slice
  11.9 0.7 add.54
  12.5 0.8 dynamic-update-slice
  13.4 25.3 %all-reduce = s32[1024]{0:T(1024)S(1)} all-reduce(s32[1024]{0:T(1024)S(1)} %dynamic-update-slice), channel_id=1, replica_groups=mesh['dp'=2,'tensor'=64] {'tensor'}, use_global_device_ids=true, to_apply=%add | all-reduce | flops 1024 | bytes 8192
  38.7 53.0 %all-gather.2.cloned.1.call-done = bf16[1024,4096]{1,0:T(8,128)(2,1)} async-done(((bf16[16,4096]{1,0:T(8,128)(2,1)}), bf16[1024,4096]{1,0:T(8,128)(2,1)}) %all-gather.2.cloned.1.call-update) | async-done | bytes 8388624 | tf_op jit(solution)/shard_map/all_gather | solution.py:46
  91.8 15.3 %fusion.13 = (f32[512]{0:T(512)S(1)}, f32[512,2004]{0,1:T(8,128)}) fusion(bf16[2004,4096]{1,0:T(8,128)(2,1)} %param.9, bf16[1024,4096]{1,0:T(8,128)(2,1)} %all-gather.2.cloned.1.call-done), kind=kOutput, calls=%fused_computation.35 | convolution fusion | flops 8406410752 | bytes 24750080 | tf_op jit(solution)/shard_map/dot_general | solution.py:14
  107.1 12.4 %fusion.14 = (f32[512]{0:T(512)S(1)}, f32[512,2004]{0,1:T(8,128)}) fusion(bf16[2004,4096]{1,0:T(8,128)(2,1)S(1)} %copy-done.3, bf16[1024,4096]{1,0:T(8,128)(2,1)} %all-gather.2.cloned.1.call-done), kind=kOutput, calls=%fused_computation.36 | convolution fusion | flops 8406410752 | bytes 24717312 | tf_op jit(solution)/shard_map/dot_general | solution.py:14
  119.5 176.9 %pmax.7 = f32[1024]{0:T(1024)S(1)} all-reduce(f32[1024]{0:T(1024)S(1)} %pad_maximum_fusion.1), channel_id=1, replica_groups=mesh['dp'=2,'tensor'=64] {'tensor'}, use_global_device_ids=true, to_apply=%region_6.7 | all-reduce | flops 1024 | bytes 8192 | tf_op jit(solution)/shard_map/pmax | solution.py:55
  296.5 0.0 copy-start.2
  296.5 0.0 copy-start.4
  296.5 5.0 fusion.4
  301.5 173.8 %all-reduce.2 = (f32[1024]{0:T(1024)S(1)}, f32[1024]{0:T(1024)S(1)}) all-reduce(f32[1024]{0:T(1024)S(1)} %pad_maximum_fusion, f32[1024]{0:T(1024)S(1)} %get-tuple-element.14), channel_id=1, replica_groups=mesh['dp'=2,'tensor'=64] {'tensor'}, use_global_device_ids=true, to_apply=%region_3.0 | all-reduce | flops 2048 | bytes 16384 | tf_op jit(solution)/shard_map/psum | solution.py:57
  475.3 0.1 convert_multiply_fusion.2
  475.4 0.0 copy-done.2
  475.4 0.2 select_reduce_fusion
  475.6 175.7 %all-reduce.1 = (f32[1024]{0:T(1024)S(1)}, f32[12]{0:T(128)S(1)}) all-reduce(f32[1024]{0:T(1024)S(1)} %get-tuple-element.13, f32[12]{0:T(128)S(1)} %select_reduce_fusion), channel_id=1, replica_groups=mesh['dp'=2,'tensor'=64] {'tensor'}, use_global_device_ids=true, to_apply=%region_12.13 | all-reduce | flops 1036 | bytes 8288 | tf_op jit(solution)/shard_map/psum | solution.py:57
  651.3 0.0 copy-done.4
  651.3 0.5 convert_divide_fusion
  651.9 0.6 subtract_multiply_fusion
  652.5 0.0 copy-done.1
  (13 shorter events, 0.1 us)
Async XLA Ops:
  7.2 84.6 %all-gather.2.cloned.1.call-start = ((), (), s32[]{:S(2)}) async-start(), calls=%async_computation | async-start | bytes 8519680 | tf_op jit(solution)/shard_map/all_gather | solution.py:46
  91.8 15.3 %copy-start.3 = (bf16[2004,4096]{1,0:T(8,128)(2,1)S(1)}, bf16[2004,4096]{1,0:T(8,128)(2,1)}, u32[]{:S(2)}) copy-start(bf16[2004,4096]{1,0:T(8,128)(2,1)} %param.9) | copy-start | bytes 49250308
  296.5 178.9 %copy-start = (s32[16]{0:T(128)S(1)}, s32[16]{0:T(128)}, u32[]{:S(2)}) copy-start(s32[16]{0:T(128)} %param.13) | copy-start | bytes 196
  296.5 178.9 %copy-start.2 = (s32[12]{0:T(128)S(1)}, s32[12]{0:T(128)}, u32[]{:S(2)}) copy-start(s32[12]{0:T(128)} %param.12) | copy-start | bytes 148
  296.5 354.9 %copy-start.4 = (s32[12]{0:T(128)S(1)}, s32[12]{0:T(128)}, u32[]{:S(2)}) copy-start(s32[12]{0:T(128)} %param.11) | copy-start | bytes 148
  475.4 177.1 %copy-start.1 = (f32[16]{0:T(128)}, f32[16]{0:T(128)S(1)}, u32[]{:S(2)}) copy-start(f32[16]{0:T(128)S(1)} %convert_multiply_fusion.2) | copy-start | bytes 196
Sparse Core Ops, SparseCore 0:
  10.8 80.8 all-gather.1
where the time goes:
time: 660 us; the launch traced here: 659 us
  blocking collectives  552 us (84%)
  waiting for transfers between devices  53.1 us (8%)
  matrix products  27.8 us (4%)
  between operations  14.8 us (2%)
  other arithmetic  9.77 us (1%)
    psum x2, blocking collectives, local(): summed = lax.psum((scaled_sum, scaled_spread, picked), 'tensor')  350 us
    pmax x1, blocking collectives, local(): global_peak = lax.pmax(row_peak, 'tensor')  177 us
    all_gather x1, waiting for transfers between devices, local(): lax.all_gather(normed, 'tensor', axis=0, tiled=True)  53 us
    dot_general x2, matrix products, row_stats(): lax.dot_general(head_weight, row_block, (((1,), (1,)), ((), ())), preferr...  27.8 us
    unnamed x1, blocking collectives  25.3 us
  transfers between devices with their start and end apart: 1, of which 1 were waited for; matrix products, arithmetic and copies ran while one was open for 0% of the time, Pallas kernels for 0%

commit v1 on v0

--- a/solution.py
+++ b/solution.py
@@ -4,6 +4,13 @@
 from jax.sharding import PartitionSpec as P
 
 epsilon = 1e-05
+
+
+def all_by_exchange(x, axis, along):
+    peers = lax.axis_size(axis)
+    blocks = jnp.stack([x for _ in range(peers)])
+    blocks = lax.all_to_all(blocks, axis, split_axis=0, concat_axis=0)
+    return jnp.concatenate(blocks, axis=along)
 
 
 def row_stats(gathered, gathered_ids, head_weight, vocab_start):
@@ -43,7 +50,7 @@
     normed = (values * lax.rsqrt(meansq + epsilon) * norm_gain[None, :]).astype(jnp.bfloat16)
     width = normed.shape[0]
     gathered, gathered_ids = (
-        lax.all_gather(normed, "tensor", axis=0, tiled=True),
+        all_by_exchange(normed, "tensor", 0),
         lax.all_gather(targets, "tensor", axis=0, tiled=True),
     )
     shard_index = lax.axis_index("tensor")

time: 660 us -> 720 us (1.091)
  blocking collectives: 552 us -> 661 us
  waiting for transfers between devices: 53.1 us -> 0.01 us
  between operations: 14.8 us -> 1.42 us
  starting transfers between devices: 0.04 us -> 11.9 us
    unnamed x1, blocking collectives: 25.3 us -> 137 us
    all_gather x1 -> x0, waiting for transfers between devices: 53 us -> none  [local(): lax.all_gather(normed, 'tensor', axis=0, tiled=True)]
    all_to_all x0 -> x1, starting transfers between devices: none -> 11.9 us  [all_by_exchange(): blocks = lax.all_to_all(blocks, axis, split_axis=0, concat_axis=0)]
  transfers between devices with their start and end apart: 1 -> 1, of which waited for: 1 -> 0; matrix products, arithmetic and copies ran while one was open for 0% -> 0% of each run, Pallas kernels for 0% -> 0%
where the time goes in v1:
time: 720 us
  blocking collectives  661 us (92%)
  matrix products  27.4 us (4%)
  starting transfers between devices  11.9 us (2%)
  local copies, waits for them, and re-layouts  9.12 us (1%)
  other arithmetic  8.43 us (1%)
    psum x2, blocking collectives, local(): summed = lax.psum((scaled_sum, scaled_spread, picked), 'tensor')  350 us
    pmax x1, blocking collectives, local(): global_peak = lax.pmax(row_peak, 'tensor')  175 us
    unnamed x1, blocking collectives  137 us
    dot_general x2, matrix products, row_stats(): lax.dot_general(head_weight, row_block, (((1,), (1,)), ((), ())), preferr...  27.4 us
  transfers between devices with their start and end apart: 1, of which 0 were waited for; matrix products, arithmetic and copies ran while one was open for 0% of the time, Pallas kernels for 0%

profile of v1, /device:TPU:0, one launch (start us, length us, event | category | flops | bytes accessed | tf_op | source)
XLA Modules:
  0.0 719.6 jit_solution(7359999379734520144)
XLA Ops:
  0.6 1.1 fusion.4
  1.7 1.0 fusion.6
  2.7 4.3 stack.2
  7.0 11.9 %all-to-all-start = ((bf16[64,16,4096]{2,1,0:T(8,128)(2,1)}), bf16[64,16,4096]{2,1,0:T(8,128)(2,1)}, u32[]{:S(2)}, u32[]{:S(2)}) async-start(bf16[64,16,4096]{2,1,0:T(8,128)(2,1)} %stack.2), calls=%async_computation | async-start | bytes 16777216 | tf_op jit(solution)/shard_map/all_to_all | solution.py:12
  18.9 0.0 copy-done.5
  18.9 0.6 dynamic-slice
  20.2 0.0 copy-done.2
  20.2 0.0 copy-done.4
  20.2 0.0 copy-done.3
  20.2 0.2 dynamic-update-slice
  20.5 137.0 %all-reduce = s32[1024]{0:T(1024)S(1)} all-reduce(s32[1024]{0:T(1024)S(1)} %dynamic-update-slice), channel_id=1, replica_groups=mesh['dp'=2,'tensor'=64] {'tensor'}, use_global_device_ids=true, to_apply=%add | all-reduce | flops 1024 | bytes 8192
  157.5 0.0 all-to-all-done
  157.5 4.0 fusion.8
  161.5 13.7 %fusion.10 = (f32[512]{0:T(512)S(1)}, f32[512,2004]{0,1:T(8,128)}) fusion(bf16[512,4096]{1,0:T(8,128)(2,1)S(1)} %bitcast.26, bf16[2004,4096]{1,0:T(8,128)(2,1)} %param.9), kind=kOutput, calls=%fused_computation.32 | convolution fusion | flops 8406410752 | bytes 24717312 | tf_op jit(solution)/shard_map/dot_general | solution.py:21
  175.2 13.7 %fusion.11 = (f32[512]{0:T(512)S(1)}, f32[512,2004]{0,1:T(8,128)}) fusion(bf16[512,4096]{1,0:T(8,128)(2,1)S(1)} %bitcast.25, bf16[2004,4096]{1,0:T(8,128)(2,1)} %param.9), kind=kOutput, calls=%fused_computation.33 | convolution fusion | flops 8406410752 | bytes 24717312 | tf_op jit(solution)/shard_map/dot_general | solution.py:21
  188.9 174.7 %pmax.7 = f32[1024]{0:T(1024)S(1)} all-reduce(f32[1024]{0:T(1024)S(1)} %pad_maximum_fusion.1), channel_id=1, replica_groups=mesh['dp'=2,'tensor'=64] {'tensor'}, use_global_device_ids=true, to_apply=%region_6.7 | all-reduce | flops 1024 | bytes 8192 | tf_op jit(solution)/shard_map/pmax | solution.py:62
  363.6 4.9 fusion
  368.6 173.9 %all-reduce.2 = (f32[1024]{0:T(1024)S(1)}, f32[1024]{0:T(1024)S(1)}) all-reduce(f32[1024]{0:T(1024)S(1)} %pad_maximum_fusion, f32[1024]{0:T(1024)S(1)} %get-tuple-element.16), channel_id=1, replica_groups=mesh['dp'=2,'tensor'=64] {'tensor'}, use_global_device_ids=true, to_apply=%region_3.0 | all-reduce | flops 2048 | bytes 16384 | tf_op jit(solution)/shard_map/psum | solution.py:64
  542.5 0.1 convert_multiply_fusion.2
  542.6 0.2 select_reduce_fusion
  542.7 175.7 %all-reduce.1 = (f32[1024]{0:T(1024)S(1)}, f32[12]{0:T(128)S(1)}) all-reduce(f32[1024]{0:T(1024)S(1)} %get-tuple-element.15, f32[12]{0:T(128)S(1)} %select_reduce_fusion), channel_id=1, replica_groups=mesh['dp'=2,'tensor'=64] {'tensor'}, use_global_device_ids=true, to_apply=%region_12.13 | all-reduce | flops 1036 | bytes 8288 | tf_op jit(solution)/shard_map/psum | solution.py:64
  718.5 0.5 convert_divide_fusion
  719.0 0.6 subtract_multiply_fusion
  719.6 0.0 copy-done.1
  (16 shorter events, 0.1 us)
Async XLA Ops:
  7.0 12.0 %copy-start.5 = (u32[128]{0:T(128)S(1)}, u32[128]{0:T(128)}, u32[]{:S(2)}) copy-start(u32[128]{0:T(128)} %constant.27) | copy-start | bytes 1540
  7.0 13.2 %copy-start.2 = (s32[12]{0:T(128)S(1)}, s32[12]{0:T(128)}, u32[]{:S(2)}) copy-start(s32[12]{0:T(128)} %param.12) | copy-start | bytes 148
  7.0 13.2 %copy-start.4 = (s32[12]{0:T(128)S(1)}, s32[12]{0:T(128)}, u32[]{:S(2)}) copy-start(s32[12]{0:T(128)} %param.11) | copy-start | bytes 148
  7.0 13.2 %copy-start.3 = (s32[16]{0:T(128)S(1)}, s32[16]{0:T(128)}, u32[]{:S(2)}) copy-start(s32[16]{0:T(128)} %param.10) | copy-start | bytes 196
  7.0 150.5 %all-to-all-start = ((bf16[64,16,4096]{2,1,0:T(8,128)(2,1)}), bf16[64,16,4096]{2,1,0:T(8,128)(2,1)}, u32[]{:S(2)}, u32[]{:S(2)}) async-start(bf16[64,16,4096]{2,1,0:T(8,128)(2,1)} %stack.2), calls=%async_computation | async-start | bytes 16777216 | tf_op jit(solution)/shard_map/all_to_all | solution.py:12
  188.9 353.6 %copy-start = (s32[16]{0:T(128)S(1)}, s32[16]{0:T(128)}, u32[]{:S(2)}) copy-start(s32[16]{0:T(128)} %param.13) | copy-start | bytes 196
  542.6 177.1 %copy-start.1 = (f32[16]{0:T(128)}, f32[16]{0:T(128)S(1)}, u32[]{:S(2)}) copy-start(f32[16]{0:T(128)S(1)} %convert_multiply_fusion.2) | copy-start | bytes 196
